TPU v7x, 256 devices: a whole 4x4x8 slice. The times are simulated.
256 devices in a mesh: tm: 32 (over x_hi, z, core), stripe: 8 (over x_lo, y).
Axes of the slice: x: 4 (x_hi: 2, x_lo: 2; x = x_hi * 2 + x_lo), y: 4, z: 8, core: 2. Of those that a mesh axis runs over, the one named last changes fastest.
Arguments:
- data_vec: float32 [128, 2, 512], P('tm', None, 'stripe'), may hold values from -6 to 6
- kernel: bfloat16 [128, 2, 512, 8192], P('tm', None, None, 'stripe'), may hold values from -0.1875 to 0.1875
- time_spectrum: float32 [128], P('tm'), may hold values from 0.25 to 2
- prior_spectrum: float32 [128, 64], replicated, may hold values from 0.05 to 1
- noise_var: float32 [512], P('stripe'), may hold values from 0.1 to 1
Outputs:
- hessian_vec: float32 [128, 2, 512], P('tm', None, 'stripe')
All inputs are finite; a program needn't handle non-finite values.
Results may differ from a plain program's by a relative error of at most 0.0022.
Values may be sent and summed in bfloat16 or wider, within the bound.
No kernel may reach another device: no remote copies, remote signals or barrier semaphores. Data moves between devices by JAX's collectives and lax.ppermute only.
A program may use at most 64 MiB of HBM per device.

v0:
```python
import math
import jax
import jax.numpy as jnp
from jax import lax
from jax.sharding import PartitionSpec as P

precise = lax.Precision.HIGHEST


def angle_tables(freq_ids, time_ids, length):
    product = freq_ids[:, None] * time_ids[None, :] % (2 * length)
    angles = product.astype(jnp.float32) * (math.pi / length)
    return (jnp.cos(angles), jnp.sin(angles))


def sine_matrix(length):
    numbers = jnp.arange(length, dtype=jnp.int32) + 1
    product = numbers[:, None] * numbers[None, :] % (2 * (length + 1))
    return jnp.sin(product.astype(jnp.float32) * (math.pi / (length + 1))) * math.sqrt(
        2.0 / (length + 1)
    )


def spectra_term(values, tm_index, time_total, count):
    steps_here = values.shape[0]
    freq_ids = jnp.arange(count, dtype=jnp.int32)
    time_ids = tm_index * steps_here + jnp.arange(steps_here, dtype=jnp.int32)
    cosine, sine_part = angle_tables(freq_ids, time_ids, time_total)
    real_part = jnp.einsum("kt,tns->kns", cosine, values, precision=precise)
    imag_part = -jnp.einsum("kt,tns->kns", sine_part, values, precision=precise)
    return jnp.stack([real_part, imag_part], 1) / math.sqrt(time_total)


def times_term(images, tm_index, time_total, count):
    freqs_here = images.shape[0]
    time_ids = jnp.arange(count, dtype=jnp.int32)
    freq_ids = tm_index * freqs_here + jnp.arange(freqs_here, dtype=jnp.int32)
    cosine, sine_part = angle_tables(freq_ids, time_ids, time_total)
    time_real = jnp.einsum("kt,kns->tns", cosine, images[:, 0], precision=precise)
    time_imag = jnp.einsum("kt,kns->tns", sine_part, images[:, 1], precision=precise)
    return (time_real - time_imag) / math.sqrt(time_total)


def grid_prior(grid_stack, row_sine, column_sine, spectrum):
    forward_grid = jnp.einsum("ai,mij->maj", row_sine, grid_stack, precision=precise)
    forward_grid = (
        jnp.einsum("maj,jb->mab", forward_grid, column_sine, precision=precise) * spectrum
    )
    backward_grid = jnp.einsum("ia,mab->mib", row_sine, forward_grid, precision=precise)
    return jnp.einsum("mib,bj->mij", backward_grid, column_sine, precision=precise)


def shards(data_vec, kernel, time_spectrum, prior_spectrum, noise_var):
    tm_index = lax.axis_index("tm")
    stripes = lax.axis_size("stripe")
    steps_here = data_vec.shape[0]
    vectors = data_vec.shape[1]
    freqs_here = kernel.shape[0]
    points_here = kernel.shape[3]
    time_total = steps_here * lax.axis_size("tm")
    rows_all = prior_spectrum.shape[0]
    columns = prior_spectrum.shape[1]
    rows_here = points_here // columns
    data_all = lax.all_gather(data_vec, "stripe", axis=2, tiled=True)
    summed = lax.psum_scatter(
        spectra_term(data_all, tm_index, time_total, freqs_here * lax.axis_size("tm")),
        "tm",
        scatter_dimension=0,
        tiled=True,
    )
    spectra = summed.astype(jnp.bfloat16)
    swapped = jnp.stack([spectra[:, 1], -spectra[:, 0]], 1)
    adj_real = jnp.einsum("kcsp,kcns->knp", kernel, spectra, preferred_element_type=jnp.float32)
    adj_imag = jnp.einsum("kcsp,kcns->knp", kernel, swapped, preferred_element_type=jnp.float32)
    adjoint = jnp.stack([adj_real, adj_imag], 1) * time_spectrum[:, None, None, None]
    row_sine = sine_matrix(rows_all)
    column_sine = sine_matrix(columns)
    item_count = freqs_here * 2 * vectors
    per_group = item_count // stripes
    grid_stack = adjoint.reshape(stripes, per_group, rows_here, columns)
    shaped = grid_prior(
        lax.all_to_all(grid_stack, "stripe", split_axis=0, concat_axis=2, tiled=True)[0],
        row_sine,
        column_sine,
        prior_spectrum,
    )
    smoothed = lax.all_to_all(
        shaped[None].astype(jnp.bfloat16), "stripe", split_axis=2, concat_axis=0, tiled=True
    ).astype(jnp.float32)
    smoothed_bf = smoothed.reshape(freqs_here, 2, vectors, points_here).astype(jnp.bfloat16)
    pair_real = jnp.stack([smoothed_bf[:, 0], -smoothed_bf[:, 1]], 1)
    pair_imag = jnp.stack([smoothed_bf[:, 1], smoothed_bf[:, 0]], 1)
    out_real = jnp.einsum("kcsp,kcnp->kns", kernel, pair_real, preferred_element_type=jnp.float32)
    out_imag = jnp.einsum("kcsp,kcnp->kns", kernel, pair_imag, preferred_element_type=jnp.float32)
    images = jnp.stack([out_real, out_imag], 1)
    time_sums = lax.psum_scatter(
        times_term(images, tm_index, time_total, steps_here * lax.axis_size("tm")),
        "tm",
        scatter_dimension=0,
        tiled=True,
    )
    result = lax.psum_scatter(time_sums, "stripe", scatter_dimension=2, tiled=True)
    return result + noise_var[None, None, :] * data_vec


def solution(mesh):
    return jax.shard_map(
        shards,
        mesh=mesh,
        in_specs=(
            P("tm", None, "stripe"),
            P("tm", None, None, "stripe"),
            P("tm"),
            P(),
            P("stripe"),
        ),
        out_specs=P("tm", None, "stripe"),
        check_vma=False,
    )
```

profile of v0, /device:TPU:4, one launch (start us, length us, event | category | flops | bytes accessed | tf_op | source)
XLA Modules:
  0.0 538.7 jit_solution(7578918533974694577)
XLA Ops:
  6.5 0.8 copy.22
  7.3 29.1 %all_gather.3 = f32[4,2,512]{0,1,2:T(2,128)S(1)} all-gather(f32[4,2,64]{0,1,2:T(2,128)S(1)} %copy.22), channel_id=1, replica_groups=mesh['tm'=32,'stripe'=8] {'stripe'}, dimensions={2}, use_global_device_ids=true | all-gather | bytes 18432 | tf_op jit(solution)/shard_map/all_gather | solution.py:64
  36.5 0.2 copy.23
  36.7 0.8 convolution_bitcast_fusion
  37.4 0.7 fusion.1
  38.2 0.1 maximum_multiply_fusion
  38.3 139.7 %all-reduce.6 = bf16[128,2,2,512]{3,0,2,1:T(8,128)(2,1)S(1)} all-reduce(f32[128,2,2,512]{3,0,2,1:T(8,128)S(1)} %maximum_multiply_fusion), channel_id=2, replica_groups=mesh['tm'=32,'stripe'=8] {'tm'}, use_global_device_ids=true, to_apply=%region_0.1.clone | all-reduce | flops 262144 | bytes 1572864
  178.0 1.3 dynamic-slice
  179.9 0.0 copy-start
  180.0 4.7 convolution_bitcast_fusion.4
  184.8 0.9 copy-done
  185.7 1.2 convolution_bitcast_fusion.3
  187.0 0.1 stack.38
  187.1 0.1 mul.152
  187.2 0.1 mul.153
  187.3 0.1 broadcast_multiply_fusion
  187.3 0.7 reshape.53
  188.1 5.3 all-to-all-start
  193.4 0.0 all-reduce.5.cloned.1.call-start
  193.4 6.3 %all-to-all-done = f32[8,1,2048]{2,1,0:T(1,128)S(1)} async-done(((f32[8,1,2048]{2,1,0:T(1,128)}), f32[8,1,2048]{2,1,0:T(1,128)S(1)}, u32[]{:S(2)}, u32[]{:S(2)}) %all-to-all-start) | async-done | bytes 65568 | tf_op jit(solution)/shard_map/all_to_all | solution.py:82
  199.7 0.5 broadcast.63
  200.2 0.8 reduce
  201.0 0.1 reshape.54
  201.1 0.6 convolution_bitcast_fusion.2
  201.7 0.4 convolution_multiply_fusion
  202.1 0.6 convolution_bitcast_fusion.1
  202.7 0.4 fusion.2
  203.1 0.1 copy.29
  203.2 0.1 reshape.55
  203.3 8.7 %all_to_all.33 = bf16[8,2,1024]{2,1,0:T(2,128)(2,1)S(1)} all-to-all(bf16[8,2,1024]{2,1,0:T(2,128)(2,1)S(1)} %reshape.55), channel_id=1, replica_groups=mesh['tm'=32,'stripe'=8] {'stripe'}, dimensions={0} | all-to-all | bytes 65536 | tf_op jit(solution)/shard_map/all_to_all | solution.py:87
  212.0 0.1 reshape.56
  212.1 0.1 reshape.44
  212.2 0.1 fusion.114
  212.4 5.7 %convolution_bitcast_fusion.6 = f32[4,2,512]{2,1,0:T(2,128)S(1)} fusion(bf16[4,2,512,1024]{3,2,1,0:T(8,128)(2,1)} %param.6, bf16[4,1,2,1024]{3,2,1,0:T(2,128)(2,1)S(1)} %get-tuple-element.5, bf16[4,1,2,1024]{3,2,1,0:T(2,128)(2,1)S(1)} %copy.48), kind=kOutput, calls=%fused_computation.13 | convolution fusion | flops 16842752 | bytes 8437760 | tf_op jit(solution)/shard_map/kcsp,kcnp->kns/dot_general | solution.py:93
  218.0 0.8 fusion.45
  218.8 5.7 %convolution_bitcast_fusion.5 = f32[4,2,512]{2,1,0:T(2,128)S(1)} fusion(bf16[4,2,512,1024]{3,2,1,0:T(8,128)(2,1)} %param.6, bf16[4,1,2,1024]{3,2,1,0:T(2,128)(2,1)S(1)} %copy.48, bf16[4,1,2,1024]{3,2,1,0:T(2,128)(2,1)S(1)} %get-tuple-element.6), kind=kOutput, calls=%fused_computation.12 | convolution fusion | flops 16842752 | bytes 8437760 | tf_op jit(solution)/shard_map/kcsp,kcnp->kns/dot_general | solution.py:94
  224.5 1.6 fusion
  226.0 0.0 all-reduce.5.cloned.1.call-update
  226.0 0.0 reduce-scatter.6.cloned.1.call-start
  226.1 262.5 %all-reduce.5.cloned.1.call-done = f32[128,2,512]{2,0,1:T(8,128)} async-done(((f32[128,2,512]{2,0,1:T(8,128)}), f32[128,2,512]{2,0,1:T(8,128)}) %all-reduce.5.cloned.1.call-update) | async-done | bytes 524304
  488.6 0.8 constant_dynamic-slice_fusion
  489.3 0.3 copy.46
  489.6 1.0 reshape.49
  490.6 0.0 reduce-scatter.6.cloned.1.call-update
  490.6 39.7 %reduce-scatter.6.cloned.1.call-done = f32[64,8]{1,0:T(8,128)} async-done(((f32[512,8]{1,0:T(8,128)}), f32[64,8]{1,0:T(8,128)}) %reduce-scatter.6.cloned.1.call-update) | async-done | bytes 2064
  530.3 0.9 reshape.50
  531.2 0.1 copy.47
  531.3 0.6 copy.35
  (21 shorter events, 0.2 us)
Async XLA Ops:
  179.9 5.8 %copy-start = (bf16[4,2,512,1024]{3,2,1,0:T(8,128)(2,1)S(1)}, bf16[4,2,512,1024]{3,2,1,0:T(8,128)(2,1)}, u32[]{:S(2)}) copy-start(bf16[4,2,512,1024]{3,2,1,0:T(8,128)(2,1)} %param.6) | copy-start | bytes 25165828
  180.0 7.1 %copy-start.3 = (f32[4]{0:T(128)S(1)}, f32[4]{0:T(128)}, u32[]{:S(2)}) copy-start(f32[4]{0:T(128)} %param.7) | copy-start | bytes 52
  180.0 21.7 %copy-start.1 = (f32[128,64]{0,1:T(8,128)S(1)}, f32[128,64]{0,1:T(8,128)}, u32[]{:S(2)}) copy-start(f32[128,64]{0,1:T(8,128)} %param.8) | copy-start | bytes 98308
  188.1 11.6 %all-to-all-start = ((f32[8,1,2048]{2,1,0:T(1,128)}), f32[8,1,2048]{2,1,0:T(1,128)S(1)}, u32[]{:S(2)}, u32[]{:S(2)}) async-start(f32[8,1,2048]{2,1,0:T(1,128)} %reshape.53), calls=%async_computation | async-start | bytes 131072 | tf_op jit(solution)/shard_map/all_to_all | solution.py:82
  193.4 295.2 %all-reduce.5.cloned.1.call-start = ((), (), s32[]{:S(2)}) async-start(), calls=%async_computation.4 | async-start | bytes 1048576
  212.4 318.9 %copy-start.2 = (f32[4,2,64]{2,1,0:T(2,128)S(1)}, f32[4,2,64]{2,1,0:T(2,128)}, u32[]{:S(2)}) copy-start(f32[4,2,64]{2,1,0:T(2,128)} %param.5) | copy-start | bytes 6148
  212.4 318.9 %copy-start.4 = (f32[64]{0:T(128)S(1)}, f32[64]{0:T(128)}, u32[]{:S(2)}) copy-start(f32[64]{0:T(128)} %param.9) | copy-start | bytes 772
  226.0 304.3 %reduce-scatter.6.cloned.1.call-start = ((), (), s32[]{:S(2)}) async-start(), calls=%async_computation.3 | async-start | bytes 294912
Sparse Core Ops, SparseCore 0:
  226.2 262.3 all-reduce.4
  491.1 39.2 reduce-scatter.5
where the time goes:
time: 539 us
  waiting for transfers between devices  308 us (57%)
  blocking collectives  177 us (33%)
  matrix products  23 us (4%)
  between operations  14.3 us (3%)
  local copies, waits for them, and re-layouts  9.02 us (2%)
    unnamed x4, waiting for transfers between devices  302 us
    unnamed x1, blocking collectives  140 us
    all_gather x1, blocking collectives, shards(): data_all = lax.all_gather(data_vec, 'stripe', axis=2, tiled=True)  29.1 us
  transfers between devices with their start and end apart: 3, of which 3 were waited for; matrix products, arithmetic and copies ran while one was open for 0% of the time, Pallas kernels for 0%

commit v1 on v0

--- a/solution.py
+++ b/solution.py
@@ -5,6 +5,13 @@
 from jax.sharding import PartitionSpec as P
 
 precise = lax.Precision.HIGHEST
+
+
+def exchange_gather(x, name, dim):
+    count = lax.axis_size(name)
+    parts = jnp.stack([x for _ in range(count)])
+    parts = lax.all_to_all(parts, name, split_axis=0, concat_axis=0)
+    return jnp.concatenate(parts, axis=dim)
 
 
 def angle_tables(freq_ids, time_ids, length):
@@ -61,7 +68,7 @@
     rows_all = prior_spectrum.shape[0]
     columns = prior_spectrum.shape[1]
     rows_here = points_here // columns
-    data_all = lax.all_gather(data_vec, "stripe", axis=2, tiled=True)
+    data_all = exchange_gather(data_vec, "stripe", 2)
     summed = lax.psum_scatter(
         spectra_term(data_all, tm_index, time_total, freqs_here * lax.axis_size("tm")),
         "tm",

time: 539 us -> 522 us (0.968)
  blocking collectives: 177 us -> 152 us
    all_gather x1 -> x0, blocking collectives: 29.1 us -> none  [shards(): data_all = lax.all_gather(data_vec, 'stripe', axis=2, tiled=True)]
  transfers between devices with their start and end apart: 3 -> 4, of which waited for: 3 -> 4; matrix products, arithmetic and copies ran while one was open for 0% -> 0% of each run, Pallas kernels for 0% -> 0%
where the time goes in v1:
time: 522 us
  waiting for transfers between devices  312 us (60%)
  blocking collectives  152 us (29%)
  matrix products  23 us (4%)
  between operations  14.3 us (3%)
  local copies, waits for them, and re-layouts  10.2 us (2%)
  starting transfers between devices  8.9 us (2%)
    unnamed x4, waiting for transfers between devices  302 us
    unnamed x1, blocking collectives  143 us
  transfers between devices with their start and end apart: 4, of which 4 were waited for; matrix products, arithmetic and copies ran while one was open for 0% of the time, Pallas kernels for 0%

profile of v1, /device:TPU:4, one launch (start us, length us, event | category | flops | bytes accessed | tf_op | source)
XLA Modules:
  0.0 521.8 jit_solution(7382762255527206914)
XLA Ops:
  6.5 0.7 copy.22
  7.2 0.7 reshape.63
  7.9 5.1 all-to-all-start
  13.1 0.7 mul.152
  13.8 0.1 mul.153
  13.9 1.3 dynamic-slice
  15.8 3.5 all-to-all-done
  19.2 0.5 broadcast.65
  19.8 0.7 reduce
  20.5 0.1 reshape.64
  20.6 0.1 reshape.43
  20.6 0.7 convolution_bitcast_fusion
  21.4 0.7 fusion.1
  22.1 0.1 maximum_multiply_fusion
  22.3 142.9 %all-reduce.6 = bf16[128,2,2,512]{3,0,2,1:T(8,128)(2,1)S(1)} all-reduce(f32[128,2,2,512]{3,0,2,1:T(8,128)S(1)} %maximum_multiply_fusion), channel_id=2, replica_groups=mesh['tm'=32,'stripe'=8] {'tm'}, use_global_device_ids=true, to_apply=%region_0.1.clone | all-reduce | flops 262144 | bytes 1572864
  165.3 4.7 convolution_bitcast_fusion.4
  170.0 0.9 copy-done
  171.0 1.2 convolution_bitcast_fusion.3
  172.2 0.1 stack.50
  172.4 0.1 broadcast_multiply_fusion
  172.5 0.7 reshape.65
  173.2 3.7 all-to-all-start.1
  177.0 6.3 %all-to-all-done.1 = f32[8,1,2048]{2,1,0:T(1,128)S(1)} async-done(((f32[8,1,2048]{2,1,0:T(1,128)}), f32[8,1,2048]{2,1,0:T(1,128)S(1)}, u32[]{:S(2)}, u32[]{:S(2)}) %all-to-all-start.1) | async-done | bytes 65568 | tf_op jit(solution)/shard_map/all_to_all | solution.py:89
  183.3 0.8 reduce.1
  184.1 0.1 reshape.66
  184.2 0.6 convolution_bitcast_fusion.2
  184.7 0.4 convolution_multiply_fusion
  185.1 0.6 convolution_bitcast_fusion.1
  185.7 0.4 fusion.2
  186.1 0.1 copy.28
  186.2 0.1 reshape.67
  186.3 8.7 %all_to_all.38 = bf16[8,2,1024]{2,1,0:T(2,128)(2,1)S(1)} all-to-all(bf16[8,2,1024]{2,1,0:T(2,128)(2,1)S(1)} %reshape.67), channel_id=1, replica_groups=mesh['tm'=32,'stripe'=8] {'stripe'}, dimensions={0} | all-to-all | bytes 65536 | tf_op jit(solution)/shard_map/all_to_all | solution.py:94
  195.0 0.1 reshape.68
  195.1 0.1 reshape.54
  195.3 0.1 fusion.113
  195.4 5.7 %convolution_bitcast_fusion.6 = f32[4,2,512]{2,1,0:T(2,128)S(1)} fusion(bf16[4,2,512,1024]{3,2,1,0:T(8,128)(2,1)} %param.6, bf16[4,1,2,1024]{3,2,1,0:T(2,128)(2,1)S(1)} %get-tuple-element.5, bf16[4,1,2,1024]{3,2,1,0:T(2,128)(2,1)S(1)} %copy.47), kind=kOutput, calls=%fused_computation.13 | convolution fusion | flops 16842752 | bytes 8437760 | tf_op jit(solution)/shard_map/kcsp,kcnp->kns/dot_general | solution.py:100
  201.1 0.8 fusion.45
  201.8 5.7 %convolution_bitcast_fusion.5 = f32[4,2,512]{2,1,0:T(2,128)S(1)} fusion(bf16[4,2,512,1024]{3,2,1,0:T(8,128)(2,1)} %param.6, bf16[4,1,2,1024]{3,2,1,0:T(2,128)(2,1)S(1)} %copy.47, bf16[4,1,2,1024]{3,2,1,0:T(2,128)(2,1)S(1)} %get-tuple-element.6), kind=kOutput, calls=%fused_computation.12 | convolution fusion | flops 16842752 | bytes 8437760 | tf_op jit(solution)/shard_map/kcsp,kcnp->kns/dot_general | solution.py:101
  207.5 1.6 fusion
  209.1 0.0 reduce-scatter.6.cloned.1.call-start
  209.1 262.5 %all-reduce.5.cloned.1.call-done = f32[128,2,512]{2,0,1:T(8,128)} async-done(((f32[128,2,512]{2,0,1:T(8,128)}), f32[128,2,512]{2,0,1:T(8,128)}) %all-reduce.5.cloned.1.call-update) | async-done | bytes 524304
  471.6 0.8 constant_dynamic-slice_fusion
  472.4 0.3 copy.45
  472.6 1.0 reshape.59
  473.7 39.7 %reduce-scatter.6.cloned.1.call-done = f32[64,8]{1,0:T(8,128)} async-done(((f32[512,8]{1,0:T(8,128)}), f32[64,8]{1,0:T(8,128)}) %reduce-scatter.6.cloned.1.call-update) | async-done | bytes 2064
  513.4 0.9 reshape.60
  514.2 0.1 copy.46
  514.3 0.6 copy.34
  (26 shorter events, 0.3 us)
Async XLA Ops:
  7.9 11.3 %all-to-all-start = ((f32[8,1,512]{2,1,0:T(1,128)}), f32[8,1,512]{2,1,0:T(1,128)S(1)}, u32[]{:S(2)}, u32[]{:S(2)}) async-start(f32[8,1,512]{2,1,0:T(1,128)} %reshape.63), calls=%async_computation | async-start | bytes 32768 | tf_op jit(solution)/shard_map/all_to_all | solution.py:13
  165.2 5.8 %copy-start = (bf16[4,2,512,1024]{3,2,1,0:T(8,128)(2,1)S(1)}, bf16[4,2,512,1024]{3,2,1,0:T(8,128)(2,1)}, u32[]{:S(2)}) copy-start(bf16[4,2,512,1024]{3,2,1,0:T(8,128)(2,1)} %param.6) | copy-start | bytes 25165828
  165.3 19.4 %copy-start.1 = (f32[128,64]{0,1:T(8,128)S(1)}, f32[128,64]{0,1:T(8,128)}, u32[]{:S(2)}) copy-start(f32[128,64]{0,1:T(8,128)} %param.8) | copy-start | bytes 98308
  173.2 10.1 %all-to-all-start.1 = ((f32[8,1,2048]{2,1,0:T(1,128)}), f32[8,1,2048]{2,1,0:T(1,128)S(1)}, u32[]{:S(2)}, u32[]{:S(2)}) async-start(f32[8,1,2048]{2,1,0:T(1,128)} %reshape.65), calls=%async_computation.1 | async-start | bytes 131072 | tf_op jit(solution)/shard_map/all_to_all | solution.py:89
  176.9 294.7 %all-reduce.5.cloned.1.call-start = ((), (), s32[]{:S(2)}) async-start(), calls=%async_computation.5 | async-start | bytes 1048576
  195.4 318.9 %copy-start.2 = (f32[4,2,64]{2,1,0:T(2,128)S(1)}, f32[4,2,64]{2,1,0:T(2,128)}, u32[]{:S(2)}) copy-start(f32[4,2,64]{2,1,0:T(2,128)} %param.5) | copy-start | bytes 6148
  195.4 318.9 %copy-start.3 = (f32[64]{0:T(128)S(1)}, f32[64]{0:T(128)}, u32[]{:S(2)}) copy-start(f32[64]{0:T(128)} %param.9) | copy-start | bytes 772
  209.1 304.3 %reduce-scatter.6.cloned.1.call-start = ((), (), s32[]{:S(2)}) async-start(), calls=%async_computation.4 | async-start | bytes 294912
Sparse Core Ops, SparseCore 0:
  209.2 262.3 all-reduce.4
  474.1 39.2 reduce-scatter.5
